TPU v7x, 256 devices: a whole 4x4x8 slice. The times are simulated.
256 devices in a mesh: energy: 64 (over x, z_hi, y), space: 4 (over z_lo, core).
Axes of the slice: x: 4, y: 4, z: 8 (z_hi: 4, z_lo: 2; z = z_hi * 2 + z_lo), core: 2. Of those that a mesh axis runs over, the one named last changes fastest.
Arguments:
- g_lesser: bfloat16 [64, 2, 4, 512, 512], P('energy', None, 'space'), may hold values from -6 to 6, as said below
- w_lesser: bfloat16 [64, 2, 4, 512, 512], P('energy', None, 'space'), may hold values from -6 to 6, as said below
- g_retarded: bfloat16 [64, 2, 4, 4, 512, 512], P('energy', None, 'space'), may hold values from -0.1875 to 0.1875
- energy_index: int32 [64], replicated, may hold values from 0 to 63, each once
Outputs:
- sigma_lesser: bfloat16 [64, 2, 4, 512, 512], P('energy', None, 'space')
- delta_green: bfloat16 [64, 2, 4, 512, 512], P('energy', None, 'space')
Inputs may be any that keep to these rules, and one draw needn't show every extreme that they name: `g_lesser`: anti-Hermitian in every diagonal block at every energy: element (j, i) of component 0 is minus element (i, j), of component 1 equal to it. `w_lesser`: anti-Hermitian in every diagonal block at every energy: element (j, i) of component 0 is minus element (i, j), of component 1 equal to it. `energy_index`: each grid point once.
All inputs are finite; a program needn't handle non-finite values.
Results may differ from a plain program's by a relative error of at most 0.013.
Values may be sent and summed in bfloat16 or wider, within the bound.
A program may use at most 128 MiB of HBM per device.

v0:
```python
import math
import jax
import jax.numpy as jnp
from jax import lax
from jax.sharding import PartitionSpec as P


def twiddles(energy_index, per_device, groups):
    grid_size = energy_index.shape[0]
    padded_len = 2 * grid_size
    row_count = 2 * grid_size
    row_ids = lax.iota(jnp.int32, row_count)
    local_energy = row_ids // (2 * groups)
    component = row_ids // groups % 2
    source = row_ids % groups
    stored = source * per_device + local_energy
    grid_point = energy_index[stored]
    frequency = lax.iota(jnp.int32, padded_len)
    forward_phase = frequency[:, None] * grid_point[None, :] % padded_len
    forward_angle = forward_phase.astype(jnp.float32) * (2.0 * math.pi / padded_len)
    cos_fwd = jnp.cos(forward_angle)
    sin_fwd = jnp.sin(forward_angle)
    real_column = (component == 0)[None, :]
    forward = jnp.concatenate(
        [jnp.where(real_column, cos_fwd, sin_fwd), jnp.where(real_column, -sin_fwd, cos_fwd)],
        axis=0,
    )
    shifted = grid_point + grid_size // 2
    backward_phase = shifted[:, None] * frequency[None, :] % padded_len
    backward_angle = backward_phase.astype(jnp.float32) * (2.0 * math.pi / padded_len)
    cos_back = jnp.cos(backward_angle)
    sin_back = jnp.sin(backward_angle)
    real_row = (component == 0)[:, None]
    factor = grid_size ** (-0.5) / padded_len
    left_half = jnp.where(real_row, -sin_back, cos_back) * factor
    right_half = jnp.where(real_row, -cos_back, -sin_back) * factor
    backward = jnp.concatenate([left_half, right_half], axis=1)
    return (forward, backward)


def transform(matrix_high, matrix_low, operand):
    return jnp.dot(matrix_high, operand, preferred_element_type=jnp.float32) + jnp.dot(
        matrix_low, operand, preferred_element_type=jnp.float32
    )


def convolve(green_rows, screen_rows, forward, backward):
    padded_len = forward.shape[0] // 2
    forward_high = forward.astype(jnp.bfloat16)
    forward_low = (forward - forward_high.astype(jnp.float32)).astype(jnp.bfloat16)
    green_hat = transform(forward_high, forward_low, green_rows)
    screen_hat = transform(forward_high, forward_low, screen_rows)
    green_real = green_hat[:padded_len]
    green_imag = green_hat[padded_len:]
    screen_real = screen_hat[:padded_len]
    screen_imag = screen_hat[padded_len:]
    prod_real = green_real * screen_real - green_imag * screen_imag
    prod_imag = green_real * screen_imag + green_imag * screen_real
    merged = jnp.concatenate([prod_real, prod_imag], axis=0)
    return jnp.dot(backward, merged, precision=lax.Precision.HIGH).astype(jnp.bfloat16)


def shards(g_lesser, w_lesser, g_retarded, energy_index):
    energies_here = g_lesser.shape[0]
    width = g_lesser.shape[3]
    groups = lax.axis_size("energy")
    forward, backward = twiddles(energy_index, energies_here, groups)
    own_row = g_retarded[:, :, 0]
    columns = width * width // groups
    green = g_lesser.reshape(energies_here, 2, groups, columns)
    screen = w_lesser.reshape(energies_here, 2, groups, columns)
    green_el, screen_el = (
        lax.all_to_all(green, "energy", split_axis=2, concat_axis=2, tiled=True),
        lax.all_to_all(screen, "energy", split_axis=2, concat_axis=2, tiled=True),
    )
    sigma_el = convolve(
        green_el.reshape(-1, columns), screen_el.reshape(-1, columns), forward, backward
    )
    sigma_el = sigma_el.reshape(energies_here, 2, groups, columns)
    sigma_back = lax.all_to_all(sigma_el, "energy", split_axis=2, concat_axis=2, tiled=True)
    sigma_lesser = sigma_back.reshape(energies_here, 2, 1, width, width)
    first_prod = jnp.einsum(
        "ecnij,ednjl->encdil",
        own_row,
        lax.all_gather(sigma_lesser, "space", axis=2, tiled=True),
        preferred_element_type=jnp.float32,
    )
    left_product = jnp.stack(
        [
            first_prod[:, :, 0, 0] - first_prod[:, :, 1, 1],
            first_prod[:, :, 0, 1] + first_prod[:, :, 1, 0],
        ],
        axis=1,
    ).astype(jnp.bfloat16)
    second_prod = jnp.einsum(
        "ecnil,ednml->ecdim", left_product, own_row, preferred_element_type=jnp.float32
    )
    out_real = second_prod[:, 0, 0] + second_prod[:, 1, 1]
    out_imag = second_prod[:, 1, 0] - second_prod[:, 0, 1]
    delta = jnp.stack([out_real, out_imag], axis=1)
    delta_green = delta.astype(jnp.bfloat16).reshape(energies_here, 2, 1, width, width)
    return (sigma_lesser, delta_green)


def solution(mesh):
    return jax.shard_map(
        shards,
        mesh=mesh,
        in_specs=(
            P("energy", None, "space", None, None),
            P("energy", None, "space", None, None),
            P("energy", None, "space", None, None, None),
            P(),
        ),
        out_specs=(P("energy", None, "space", None, None), P("energy", None, "space", None, None)),
        check_vma=False,
    )
```

profile of v0, /device:TPU:1, one launch (start us, length us, event | category | flops | bytes accessed | tf_op | source)
XLA Modules:
  0.0 215.1 jit_solution(1046797866290290498)
XLA Ops:
  7.2 0.0 copy-start
  7.2 0.0 copy-start.4
  7.2 1.6 reshape.274
  8.8 2.1 copy.28
  10.9 15.1 %all-to-all-start.1 = ((bf16[1,2,64,4096]{3,1,0,2:T(2,128)(2,1)}), bf16[1,2,64,4096]{3,1,0,2:T(2,128)(2,1)S(1)}, u32[]{:S(2)}, u32[]{:S(2)}) async-start(bf16[1,2,64,4096]{3,1,0,2:T(2,128)(2,1)} %copy.28), calls=%async_computation.1 | async-start | bytes 2097152 | tf_op jit(solution)/shard_map/all_to_all | solution.py:74
  26.0 0.0 copy-done.4
  26.0 0.5 reshape.272
  26.6 2.1 copy.26
  28.6 25.1 %all-to-all-done.1 = bf16[1,2,64,4096]{3,1,0,2:T(2,128)(2,1)S(1)} async-done(((bf16[1,2,64,4096]{3,1,0,2:T(2,128)(2,1)}), bf16[1,2,64,4096]{3,1,0,2:T(2,128)(2,1)S(1)}, u32[]{:S(2)}, u32[]{:S(2)}) %all-to-all-start.1) | async-done | bytes 1048608 | tf_op jit(solution)/shard_map/all_to_all | solution.py:74
  53.7 8.3 %all-to-all-start = ((bf16[1,2,64,4096]{3,1,0,2:T(2,128)(2,1)}), bf16[1,2,64,4096]{3,1,0,2:T(2,128)(2,1)S(1)}, u32[]{:S(2)}, u32[]{:S(2)}) async-start(bf16[1,2,64,4096]{3,1,0,2:T(2,128)(2,1)} %copy.26), calls=%async_computation | async-start | bytes 2097152 | tf_op jit(solution)/shard_map/all_to_all | solution.py:73
  62.0 0.2 all-gather.2.cloned.1.call-start
  62.3 0.0 copy-done
  62.3 1.2 gather_fusion
  63.6 0.6 select_multiply_fusion.1
  64.2 0.6 copy.29
  64.8 0.7 fusion.36
  65.5 2.6 %convolution_add_fusion = f32[256,4096]{1,0:T(8,128)} fusion(f32[256,4096]{1,0:T(8,128)S(1)} %fusion.36, bf16[128,4096]{1,0:T(8,128)(2,1)S(1)} %bitcast.74, f32[128,128]{1,0:T(8,128)S(1)} %get-tuple-element.18, f32[128,128]{1,0:T(8,128)S(1)} %get-tuple-element.19), kind=kOutput, calls=%fused_computation.2 | convolution fusion | flops 269647872 | bytes 9568256 | tf_op jit(solution)/shard_map/dot_general | solution.py:42
  68.1 22.7 %all-to-all-done = bf16[1,2,64,4096]{3,1,0,2:T(2,128)(2,1)S(1)} async-done(((bf16[1,2,64,4096]{3,1,0,2:T(2,128)(2,1)}), bf16[1,2,64,4096]{3,1,0,2:T(2,128)(2,1)S(1)}, u32[]{:S(2)}, u32[]{:S(2)}) %all-to-all-start) | async-done | bytes 1048608 | tf_op jit(solution)/shard_map/all_to_all | solution.py:73
  90.8 0.6 copy.27
  91.3 0.7 fusion.38
  92.0 0.0 copy-start.2
  92.0 0.7 convolution_add_fusion.1
  92.8 1.5 copy-done.2
  94.2 0.9 multiply_subtract_fusion
  95.2 1.5 convolution_convert_fusion
  96.7 1.1 copy.30
  97.8 32.1 %all_to_all.15 = bf16[1,2,64,4096]{3,1,0,2:T(2,128)(2,1)S(1)} all-to-all(bf16[1,2,64,4096]{3,1,0,2:T(2,128)(2,1)S(1)} %copy.30), channel_id=1, replica_groups=mesh['energy'=64,'space'=4] {'energy'}, dimensions={2} | all-to-all | bytes 2097152 | tf_op jit(solution)/shard_map/all_to_all | solution.py:80
  130.0 0.6 copy.31
  130.6 1.3 reshape.277
  131.9 0.0 all-gather.2.cloned.1.call-update
  131.9 47.4 %all-gather.2.cloned.1.call-done = bf16[1,2,4,512,512]{4,3,1,0,2:T(8,128)(2,1)} async-done(((bf16[1,2,1,512,512]{4,3,1,0,2:T(8,128)(2,1)}), bf16[1,2,4,512,512]{4,3,1,0,2:T(8,128)(2,1)}) %all-gather.2.cloned.1.call-update) | async-done | bytes 4194320 | tf_op jit(solution)/shard_map/all_gather | solution.py:85
  179.3 14.1 %convolution_bitcast_fusion = f32[1,4,2,2,512,512]{4,5,2,3,1,0:T(8,128)} fusion(bf16[1,2,4,512,512]{4,3,1,0,2:T(8,128)(2,1)} %all-gather.2.cloned.1.call-done, bf16[1,2,1,4,512,512]{5,4,3,2,1,0:T(8,128)(2,1)} %param.6), kind=kOutput, calls=%fused_computation.1 | convolution fusion | flops 4294967296 | bytes 25165824 | tf_op jit(solution)/shard_map/ecnij,ednjl->encdil/dot_general | solution.py:82
  193.4 4.2 %fusion.13 = bf16[1,4,512,512]{2,3,1,0:T(8,128)(2,1)S(1)} fusion(f32[1,4,2,2,512,512]{4,5,2,3,1,0:T(8,128)} %convolution_bitcast_fusion), kind=kLoop, calls=%fused_computation.22 | loop fusion | flops 2097152 | bytes 10485760 | tf_op jit(solution)/shard_map/add | solution.py:91
  197.6 0.0 copy-start.3
  197.6 4.4 %fusion.12 = bf16[1,4,512,512]{2,3,1,0:T(8,128)(2,1)S(1)} fusion(f32[1,4,2,2,512,512]{4,5,2,3,1,0:T(8,128)} %convolution_bitcast_fusion), kind=kLoop, calls=%fused_computation.21 | loop fusion | flops 2097152 | bytes 10485760 | tf_op jit(solution)/shard_map/sub | solution.py:90
  202.1 0.2 copy-done.3
  202.3 0.0 copy-start.1
  202.3 4.5 %fusion.11 = f32[1,2,2,512,512]{4,3,2,1,0:T(8,128)S(1)} fusion(bf16[1,4,512,512]{2,3,1,0:T(8,128)(2,1)S(1)} %fusion.13, bf16[1,4,512,512]{2,3,1,0:T(8,128)(2,1)S(1)} %fusion.12, bf16[1,2,1,4,512,512]{5,4,3,2,1,0:T(8,128)(2,1)S(1)} %copy-done.3), kind=kOutput, calls=%fused_computation.20 | convolution fusion | flops 4303355904 | bytes 12582912 | tf_op jit(solution)/shard_map/ecnil,ednml->ecdim/dot_general | solution.py:95
  206.8 0.4 fusion.15
  207.2 1.1 pad_maximum_fusion
  208.2 0.0 copy-done.1
  (4 shorter events, 0.0 us)
Async XLA Ops:
  7.2 55.1 %copy-start = (s32[64]{0:T(128)S(1)}, s32[64]{0:T(128)}, u32[]{:S(2)}) copy-start(s32[64]{0:T(128)} %param.7) | copy-start | bytes 772
  7.2 18.8 %copy-start.4 = (bf16[1,2,1,512,512]{4,3,2,1,0:T(8,128)(2,1)S(1)}, bf16[1,2,1,512,512]{4,3,2,1,0:T(8,128)(2,1)}, u32[]{:S(2)}) copy-start(bf16[1,2,1,512,512]{4,3,2,1,0:T(8,128)(2,1)} %param.4) | copy-start | bytes 3145732
  10.9 42.8 %all-to-all-start.1 = ((bf16[1,2,64,4096]{3,1,0,2:T(2,128)(2,1)}), bf16[1,2,64,4096]{3,1,0,2:T(2,128)(2,1)S(1)}, u32[]{:S(2)}, u32[]{:S(2)}) async-start(bf16[1,2,64,4096]{3,1,0,2:T(2,128)(2,1)} %copy.28), calls=%async_computation.1 | async-start | bytes 2097152 | tf_op jit(solution)/shard_map/all_to_all | solution.py:74
  53.7 37.0 %all-to-all-start = ((bf16[1,2,64,4096]{3,1,0,2:T(2,128)(2,1)}), bf16[1,2,64,4096]{3,1,0,2:T(2,128)(2,1)S(1)}, u32[]{:S(2)}, u32[]{:S(2)}) async-start(bf16[1,2,64,4096]{3,1,0,2:T(2,128)(2,1)} %copy.26), calls=%async_computation | async-start | bytes 2097152 | tf_op jit(solution)/shard_map/all_to_all | solution.py:73
  62.0 117.3 %all-gather.2.cloned.1.call-start = ((), (), s32[]{:S(2)}) async-start(), calls=%async_computation.3 | async-start | bytes 5242880 | tf_op jit(solution)/shard_map/all_gather | solution.py:85
  92.0 2.2 %copy-start.2 = (f32[256,4096]{1,0:T(8,128)S(1)}, f32[256,4096]{1,0:T(8,128)}, u32[]{:S(2)}) copy-start(f32[256,4096]{1,0:T(8,128)} %convolution_add_fusion) | copy-start | bytes 12582916
  197.6 4.6 %copy-start.3 = (bf16[1,2,1,4,512,512]{5,4,3,2,1,0:T(8,128)(2,1)S(1)}, bf16[1,2,1,4,512,512]{5,4,3,2,1,0:T(8,128)(2,1)}, u32[]{:S(2)}) copy-start(bf16[1,2,1,4,512,512]{5,4,3,2,1,0:T(8,128)(2,1)} %param.6) | copy-start | bytes 12582916
  202.3 6.0 %copy-start.1 = (s32[64]{0:T(128)S(1)}, s32[64]{0:T(128)}, u32[]{:S(2)}) copy-start(s32[64]{0:T(128)} %param.7) | copy-start | bytes 772
Sparse Core Ops, SparseCore 0:
  132.0 47.2 all-gather.1
where the time goes:
time: 215 us
  waiting for transfers between devices  95.2 us (44%)
  blocking collectives  32.1 us (15%)
  matrix products  24.9 us (12%)
  starting transfers between devices  23.7 us (11%)
  between operations  14.2 us (7%)
  local copies, waits for them, and re-layouts  13.4 us (6%)
  other arithmetic  11.6 us (5%)
    all_gather x1, waiting for transfers between devices, shards(): lax.all_gather(sigma_lesser, 'space', axis=2, tiled=True)  47.4 us
    all_to_all x1, blocking collectives, shards(): lax.all_to_all(sigma_el, 'energy', split_axis=2, concat_axis=2, tiled=True)  32.1 us
    all_to_all x1, waiting for transfers between devices, shards(): lax.all_to_all(screen, 'energy', split_axis=2, concat_axis=2, tiled=True)  25.1 us
    all_to_all x1, waiting for transfers between devices, shards(): lax.all_to_all(green, 'energy', split_axis=2, concat_axis=2, tiled=True)  22.7 us
    all_to_all x1, starting transfers between devices, shards(): lax.all_to_all(screen, 'energy', split_axis=2, concat_axis=2, tiled=True)  15.1 us
    dot_general x1, matrix products, shards(): jnp.einsum('ecnij,ednjl->encdil', own_row, lax.all_gather(sigma_lesser, '...  14.1 us
    all_to_all x1, starting transfers between devices, shards(): lax.all_to_all(green, 'energy', split_axis=2, concat_axis=2, tiled=True)  8.33 us
    dot_general x1, matrix products, shards(): jnp.einsum('ecnil,ednml->ecdim', left_product, own_row, preferred_element...  4.54 us
  transfers between devices with their start and end apart: 3, of which 3 were waited for; matrix products, arithmetic and copies ran while one was open for 4% of the time, Pallas kernels for 0%

commit v1 on v0

--- a/solution.py
+++ b/solution.py
@@ -82,7 +82,15 @@
     first_prod = jnp.einsum(
         "ecnij,ednjl->encdil",
         own_row,
-        lax.all_gather(sigma_lesser, "space", axis=2, tiled=True),
+        jnp.concatenate(
+            lax.all_to_all(
+                jnp.stack(lax.axis_size("space") * [sigma_lesser]),
+                split_axis=0,
+                axis_name="space",
+                concat_axis=0,
+            ),
+            axis=2,
+        ),
         preferred_element_type=jnp.float32,
     )
     left_product = jnp.stack(

time: 215 us -> 201 us (0.935)
  between operations: 14.2 us -> 0.85 us
  starting transfers between devices: 23.7 us -> 32.1 us
  other arithmetic: 11.6 us -> 4.62 us
  matrix products: 24.9 us -> 18.4 us
  local copies, waits for them, and re-layouts: 13.4 us -> 17.9 us
    all_gather x1 -> x0, waiting for transfers between devices: 47.4 us -> none  [shards(): lax.all_gather(sigma_lesser, 'space', axis=2, tiled=True)]
    all_to_all x0 -> x1, waiting for transfers between devices: none -> 45.6 us  [shards(): lax.all_to_all(jnp.stack(lax.axis_size('space') * [sigma_lesser]), split_...]
    all_to_all x0 -> x1, starting transfers between devices: none -> 8.45 us  [shards(): lax.all_to_all(jnp.stack(lax.axis_size('space') * [sigma_lesser]), split_...]
    dot_general x1, matrix products: 14.1 us -> 7.61 us  [shards(): jnp.einsum('ecnij,ednjl->encdil', own_row, jnp.concatenate(lax.all_to_all...]
    sub x1, other arithmetic: 4.42 us -> 0.89 us  [shards(): first_prod[:, :, 0, 0] - first_prod[:, :, 1, 1]]
    add x1, other arithmetic: 4.19 us -> 0.75 us  [shards(): first_prod[:, :, 0, 1] + first_prod[:, :, 1, 0]]
    another operation x0 -> x3, local copies, waits for them, and re-layouts: none -> 3.42 us  [shards(): jnp.stack(lax.axis_size('space') * [sigma_lesser])]
  transfers between devices with their start and end apart: 3 -> 3, of which waited for: 3 -> 3; matrix products, arithmetic and copies ran while one was open for 4% -> 5% of each run, Pallas kernels for 0% -> 0%
where the time goes in v1:
time: 201 us; the launch traced here: 199 us
  waiting for transfers between devices  93.3 us (46%)
  starting transfers between devices  32.1 us (16%)
  blocking collectives  32.1 us (16%)
  matrix products  18.4 us (9%)
  local copies, waits for them, and re-layouts  17.9 us (9%)
  other arithmetic  4.62 us (2%)
    all_to_all x1, waiting for transfers between devices, shards(): lax.all_to_all(jnp.stack(lax.axis_size('space') * [sigma_lesser]), split_...  45.6 us
    all_to_all x1, blocking collectives, shards(): lax.all_to_all(sigma_el, 'energy', split_axis=2, concat_axis=2, tiled=True)  32.1 us
    all_to_all x1, waiting for transfers between devices, shards(): lax.all_to_all(screen, 'energy', split_axis=2, concat_axis=2, tiled=True)  25.1 us
    all_to_all x1, waiting for transfers between devices, shards(): lax.all_to_all(green, 'energy', split_axis=2, concat_axis=2, tiled=True)  22.7 us
    all_to_all x1, starting transfers between devices, shards(): lax.all_to_all(screen, 'energy', split_axis=2, concat_axis=2, tiled=True)  15.1 us
    all_to_all x1, starting transfers between devices, shards(): lax.all_to_all(green, 'energy', split_axis=2, concat_axis=2, tiled=True)  8.51 us
    all_to_all x1, starting transfers between devices, shards(): lax.all_to_all(jnp.stack(lax.axis_size('space') * [sigma_lesser]), split_...  8.45 us
    dot_general x1, matrix products, shards(): jnp.einsum('ecnij,ednjl->encdil', own_row, jnp.concatenate(lax.all_to_all...  7.61 us
  transfers between devices with their start and end apart: 3, of which 3 were waited for; matrix products, arithmetic and copies ran while one was open for 5% of the time, Pallas kernels for 0%

profile of v1, /device:TPU:1, one launch (start us, length us, event | category | flops | bytes accessed | tf_op | source)
XLA Modules:
  0.0 199.3 jit_solution(15464339068481596458)
XLA Ops:
  0.6 0.0 copy-start
  0.6 0.0 copy-start.4
  0.7 1.6 reshape.283
  2.3 2.1 %copy.24 = bf16[1,2,64,4096]{3,1,0,2:T(2,128)(2,1)} copy(bf16[1,2,64,4096]{3,2,1,0:T(8,128)(2,1)S(1)} %reshape.283) | data formatting | bytes 2097152 | tf_op jit(solution)/shard_map/reshape | solution.py:71
  4.4 15.1 %all-to-all-start.1 = ((bf16[1,2,64,4096]{3,1,0,2:T(2,128)(2,1)}), bf16[1,2,64,4096]{3,1,0,2:T(2,128)(2,1)S(1)}, u32[]{:S(2)}, u32[]{:S(2)}) async-start(bf16[1,2,64,4096]{3,1,0,2:T(2,128)(2,1)} %copy.24), calls=%async_computation.1 | async-start | bytes 2097152 | tf_op jit(solution)/shard_map/all_to_all | solution.py:74
  19.5 0.0 copy-done.4
  19.5 0.5 reshape.281
  20.0 2.1 %copy.22 = bf16[1,2,64,4096]{3,1,0,2:T(2,128)(2,1)} copy(bf16[1,2,64,4096]{3,2,1,0:T(8,128)(2,1)S(1)} %reshape.281) | data formatting | bytes 2097152 | tf_op jit(solution)/shard_map/reshape | solution.py:70
  22.1 25.1 %all-to-all-done.1 = bf16[1,2,64,4096]{3,1,0,2:T(2,128)(2,1)S(1)} async-done(((bf16[1,2,64,4096]{3,1,0,2:T(2,128)(2,1)}), bf16[1,2,64,4096]{3,1,0,2:T(2,128)(2,1)S(1)}, u32[]{:S(2)}, u32[]{:S(2)}) %all-to-all-start.1) | async-done | bytes 1048608 | tf_op jit(solution)/shard_map/all_to_all | solution.py:74
  47.2 8.5 %all-to-all-start = ((bf16[1,2,64,4096]{3,1,0,2:T(2,128)(2,1)}), bf16[1,2,64,4096]{3,1,0,2:T(2,128)(2,1)S(1)}, u32[]{:S(2)}, u32[]{:S(2)}) async-start(bf16[1,2,64,4096]{3,1,0,2:T(2,128)(2,1)} %copy.22), calls=%async_computation | async-start | bytes 2097152 | tf_op jit(solution)/shard_map/all_to_all | solution.py:73
  55.7 0.0 copy-done
  55.7 1.2 gather_fusion
  57.0 0.6 select_multiply_fusion.1
  57.6 0.6 copy.25
  58.2 0.7 fusion.36
  58.9 2.6 %convolution_add_fusion = f32[256,4096]{1,0:T(8,128)} fusion(f32[256,4096]{1,0:T(8,128)S(1)} %fusion.36, bf16[128,4096]{1,0:T(8,128)(2,1)S(1)} %bitcast.79, f32[128,128]{1,0:T(8,128)S(1)} %get-tuple-element.12, f32[128,128]{1,0:T(8,128)S(1)} %get-tuple-element.13), kind=kOutput, calls=%fused_computation.2 | convolution fusion | flops 269647872 | bytes 9568256 | tf_op jit(solution)/shard_map/dot_general | solution.py:42
  61.5 22.7 %all-to-all-done = bf16[1,2,64,4096]{3,1,0,2:T(2,128)(2,1)S(1)} async-done(((bf16[1,2,64,4096]{3,1,0,2:T(2,128)(2,1)}), bf16[1,2,64,4096]{3,1,0,2:T(2,128)(2,1)S(1)}, u32[]{:S(2)}, u32[]{:S(2)}) %all-to-all-start) | async-done | bytes 1048608 | tf_op jit(solution)/shard_map/all_to_all | solution.py:73
  84.2 0.6 copy.23
  84.8 0.7 fusion.38
  85.5 0.0 copy-start.2
  85.5 0.7 convolution_add_fusion.1
  86.2 1.5 copy-done.2
  87.7 0.9 multiply_subtract_fusion
  88.6 1.5 convolution_convert_fusion
  90.2 1.1 copy.26
  91.3 32.1 %all_to_all.20 = bf16[1,2,64,4096]{3,1,0,2:T(2,128)(2,1)S(1)} all-to-all(bf16[1,2,64,4096]{3,1,0,2:T(2,128)(2,1)S(1)} %copy.26), channel_id=1, replica_groups=mesh['energy'=64,'space'=4] {'energy'}, dimensions={2} | all-to-all | bytes 2097152 | tf_op jit(solution)/shard_map/all_to_all | solution.py:80
  123.4 0.6 copy.27
  124.0 0.5 stack_reshape.2
  124.6 0.5 copy.29
  125.1 2.3 %stack.6 = bf16[4,1,2,1,512,512]{4,5,2,3,1,0:T(8,128)(2,1)} broadcast(bf16[2,512,512]{1,2,0:T(8,128)(2,1)S(1)} %copy.29), dimensions={2,4,5} | broadcast | bytes 5242880 | tf_op jit(solution)/shard_map/stack | solution.py:87
  127.5 8.5 %all-to-all-start.3 = ((bf16[4,1,2,1,512,512]{4,5,2,3,1,0:T(8,128)(2,1)}), bf16[4,1,2,1,512,512]{4,5,2,3,1,0:T(8,128)(2,1)}, u32[]{:S(2)}, u32[]{:S(2)}) async-start(bf16[4,1,2,1,512,512]{4,5,2,3,1,0:T(8,128)(2,1)} %stack.6), calls=%async_computation.3 | async-start | bytes 8388608 | tf_op jit(solution)/shard_map/all_to_all | solution.py:86
  135.9 1.3 reshape.286
  137.2 45.6 %all-to-all-done.3 = bf16[4,1,2,1,512,512]{4,5,2,3,1,0:T(8,128)(2,1)} async-done(((bf16[4,1,2,1,512,512]{4,5,2,3,1,0:T(8,128)(2,1)}), bf16[4,1,2,1,512,512]{4,5,2,3,1,0:T(8,128)(2,1)}, u32[]{:S(2)}, u32[]{:S(2)}) %all-to-all-start.3) | async-done | bytes 4194336 | tf_op jit(solution)/shard_map/all_to_all | solution.py:86
  182.8 7.6 %convolution_bitcast_fusion = f32[1,4,2,2,512,512]{4,5,2,3,1,0:T(8,128)S(1)} fusion(bf16[4,1,2,1,512,512]{4,5,2,3,1,0:T(8,128)(2,1)} %all-to-all-done.3, bf16[1,2,1,4,512,512]{5,4,3,2,1,0:T(8,128)(2,1)} %param.6), kind=kOutput, calls=%fused_computation.1 | convolution fusion | flops 4294967296 | bytes 25165824 | tf_op jit(solution)/shard_map/ecnij,ednjl->encdil/dot_general | solution.py:82
  190.4 0.8 fusion.13
  191.1 0.0 copy-start.3
  191.1 0.9 fusion.12
  192.0 1.3 copy-done.3
  193.3 0.0 copy-start.1
  193.3 4.5 %fusion.11 = f32[1,2,2,512,512]{4,3,2,1,0:T(8,128)S(1)} fusion(bf16[1,4,512,512]{2,3,1,0:T(8,128)(2,1)S(1)} %fusion.13, bf16[1,4,512,512]{2,3,1,0:T(8,128)(2,1)S(1)} %fusion.12, bf16[1,2,1,4,512,512]{5,4,3,2,1,0:T(8,128)(2,1)S(1)} %copy-done.3), kind=kOutput, calls=%fused_computation.20 | convolution fusion | flops 4303355904 | bytes 12582912 | tf_op jit(solution)/shard_map/ecnil,ednml->ecdim/dot_general | solution.py:103
  197.9 0.4 fusion.15
  198.2 1.1 pad_maximum_fusion
  199.3 0.0 copy-done.1
  (4 shorter events, 0.0 us)
Async XLA Ops:
  0.6 55.1 %copy-start = (s32[64]{0:T(128)S(1)}, s32[64]{0:T(128)}, u32[]{:S(2)}) copy-start(s32[64]{0:T(128)} %param.7) | copy-start | bytes 772
  0.6 18.8 %copy-start.4 = (bf16[1,2,1,512,512]{4,3,2,1,0:T(8,128)(2,1)S(1)}, bf16[1,2,1,512,512]{4,3,2,1,0:T(8,128)(2,1)}, u32[]{:S(2)}) copy-start(bf16[1,2,1,512,512]{4,3,2,1,0:T(8,128)(2,1)} %param.4) | copy-start | bytes 3145732
  4.4 42.8 %all-to-all-start.1 = ((bf16[1,2,64,4096]{3,1,0,2:T(2,128)(2,1)}), bf16[1,2,64,4096]{3,1,0,2:T(2,128)(2,1)S(1)}, u32[]{:S(2)}, u32[]{:S(2)}) async-start(bf16[1,2,64,4096]{3,1,0,2:T(2,128)(2,1)} %copy.24), calls=%async_computation.1 | async-start | bytes 2097152 | tf_op jit(solution)/shard_map/all_to_all | solution.py:74
  47.2 37.0 %all-to-all-start = ((bf16[1,2,64,4096]{3,1,0,2:T(2,128)(2,1)}), bf16[1,2,64,4096]{3,1,0,2:T(2,128)(2,1)S(1)}, u32[]{:S(2)}, u32[]{:S(2)}) async-start(bf16[1,2,64,4096]{3,1,0,2:T(2,128)(2,1)} %copy.22), calls=%async_computation | async-start | bytes 2097152 | tf_op jit(solution)/shard_map/all_to_all | solution.py:73
  85.5 2.2 %copy-start.2 = (f32[256,4096]{1,0:T(8,128)S(1)}, f32[256,4096]{1,0:T(8,128)}, u32[]{:S(2)}) copy-start(f32[256,4096]{1,0:T(8,128)} %convolution_add_fusion) | copy-start | bytes 12582916
  127.5 55.3 %all-to-all-start.3 = ((bf16[4,1,2,1,512,512]{4,5,2,3,1,0:T(8,128)(2,1)}), bf16[4,1,2,1,512,512]{4,5,2,3,1,0:T(8,128)(2,1)}, u32[]{:S(2)}, u32[]{:S(2)}) async-start(bf16[4,1,2,1,512,512]{4,5,2,3,1,0:T(8,128)(2,1)} %stack.6), calls=%async_computation.3 | async-start | bytes 8388608 | tf_op jit(solution)/shard_map/all_to_all | solution.py:86
  191.1 2.2 %copy-start.3 = (bf16[1,2,1,4,512,512]{5,4,3,2,1,0:T(8,128)(2,1)S(1)}, bf16[1,2,1,4,512,512]{5,4,3,2,1,0:T(8,128)(2,1)}, u32[]{:S(2)}) copy-start(bf16[1,2,1,4,512,512]{5,4,3,2,1,0:T(8,128)(2,1)} %param.6) | copy-start | bytes 12582916
  193.3 6.0 %copy-start.1 = (s32[64]{0:T(128)S(1)}, s32[64]{0:T(128)}, u32[]{:S(2)}) copy-start(s32[64]{0:T(128)} %param.7) | copy-start | bytes 772
